TPU v7x, 32 devices: a whole 2x2x4 slice. The times are simulated.
32 devices in a mesh: seq: 4 (over x, core), head: 8 (over z, y).
Axes of the slice: x: 2, y: 2, z: 4, core: 2. Of those that a mesh axis runs over, the one named last changes fastest.
Arguments:
- features: bfloat16 [16384, 12288], P(('seq', 'head')), may hold values from -6 to 6
- selector: bfloat16 [16384, 256], P(('seq', 'head')), may hold values from -6 to 6
- step_input: bfloat16 [16384, 96], P(('seq', 'head')), may hold values from -2 to 20
- feature_kernel: float32 [4, 12288], replicated, may hold values from -3 to 3
- selector_kernel: float32 [4, 256], replicated, may hold values from -3 to 3
- feature_offset: float32 [12288], replicated, may hold values from -3 to 3
- selector_offset: float32 [256], replicated, may hold values from -3 to 3
- decay_log: float32 [96], replicated, may hold values from -2.4 to 0.1
- step_offset: float32 [96], replicated, may hold values from -12 to -2
- skip_scale: float32 [96], replicated, may hold values from 0.5 to 1.5
- norm_gain: float32 [12288], replicated, may hold values from 0.5 to 1.5
Outputs:
- output: bfloat16 [16384, 12288], P(('seq', 'head'))
All inputs are finite; a program needn't handle non-finite values.
Results may differ from a plain program's by a relative error of at most 0.008.
Values may be sent and summed in bfloat16 or wider, within the bound.
No kernel may reach another device: no remote copies, remote signals or barrier semaphores. Data moves between devices by JAX's collectives and lax.ppermute only.
A program may use at most 192 MiB of HBM per device.

v0:
```python
import math
import jax
import jax.numpy as jnp
from jax import lax
from jax.sharding import PartitionSpec as P

SPAN = 256


def passed_along(shard, axis, by):
    peers = lax.axis_size(axis)
    pairs = [(i, i + by) for i in range(peers) if 0 <= i + by < peers]
    return lax.ppermute(shard, axis, pairs)


def entering_2(shard, axis, join, neutral):
    place = lax.axis_index(axis)
    gathered = jax.tree.map(
        lambda a, kind: lax.all_gather(a.astype(kind), axis), shard, (jnp.bfloat16, jnp.bfloat16)
    )
    state = jax.tree.map(lambda a, e: jnp.zeros_like(a) + jnp.asarray(e, a.dtype), shard, neutral)

    def one(turn, state):
        return join(
            state,
            jax.tree.map(
                lambda a, own: lax.dynamic_index_in_dim(a, turn, 0, False).astype(own.dtype),
                gathered,
                shard,
            ),
        )

    return lax.fori_loop(0, place, one, state)


def causal_filter(tail_rows, new_rows, kernel, offset):
    length = new_rows.shape[0]
    window = jnp.concatenate([tail_rows, new_rows], axis=0).astype(jnp.float32)
    summed = jnp.broadcast_to(offset[None, :], (length, offset.shape[0]))
    for delay_step in range(kernel.shape[0]):
        summed = summed + kernel[delay_step][None, :] * window[delay_step : delay_step + length]
    return jax.nn.silu(summed).astype(jnp.bfloat16)


def normalize(values, norm_gain):
    widened = values.astype(jnp.float32)
    square = jnp.mean(widened * widened, axis=-1, keepdims=True)
    return (widened * lax.rsqrt(square + 1e-05) * norm_gain[None, :]).astype(jnp.bfloat16)


def join_states(former, latter):
    return (former[0] + latter[0], jnp.exp(latter[0])[:, None, None] * former[1] + latter[1])


def span_terms(feature_matrix_rows, write_rows, read_rows, step_size, log_decay):
    length = feature_matrix_rows.shape[0]
    head_count = step_size.shape[1]
    head_view = feature_matrix_rows.reshape(length, head_count, -1)
    cumulative = jnp.cumsum(log_decay, axis=0)
    inputs = (step_size[:, :, None] * head_view).astype(jnp.bfloat16)
    scores = jnp.dot(read_rows, write_rows.T, preferred_element_type=jnp.float32)
    log_spacing = cumulative.T[:, :, None] - cumulative.T[:, None, :]
    causal = jnp.arange(length)[:, None] >= jnp.arange(length)[None, :]
    decay_mask = jnp.exp(jnp.where(causal[None], log_spacing, -jnp.inf))
    mixing = (scores[None] * decay_mask).astype(jnp.bfloat16)
    diagonal = jnp.einsum("hij,jhp->ihp", mixing, inputs, preferred_element_type=jnp.float32)
    log_total = cumulative[-1]
    weighted = (
        (step_size * jnp.exp(log_total[None, :] - cumulative))[:, :, None] * head_view
    ).astype(jnp.bfloat16)
    span_state = jnp.einsum("jn,jhp->hnp", write_rows, weighted, preferred_element_type=jnp.float32)
    return (diagonal, cumulative, span_state, log_total)


def group_spans(values, span_count, group_size):
    return values.reshape((span_count // group_size, group_size, SPAN) + values.shape[1:])


def ungroup(values, span_count):
    return values.reshape((span_count,) + values.shape[2:])


def chain_states(span_states, log_totals):

    def advance(running, record):
        span_state, log_total = record
        return (jnp.exp(log_total)[:, None, None] * running + span_state, running)

    final_state, entering = lax.scan(
        advance, jnp.zeros_like(span_states[0]), (span_states, log_totals)
    )
    before = jnp.cumsum(log_totals, axis=0) - log_totals
    return (entering, before, final_state, jnp.sum(log_totals, axis=0))


def selective_rows(
    feature_conv, selector_conv, step_rows, decay_log, step_offset, skip_scale, carry_fn
):
    state_size = selector_conv.shape[1] // 2
    row_count = feature_conv.shape[0]
    span_count = row_count // SPAN
    group_size = math.gcd(span_count, 8)
    step_size = jax.nn.softplus(step_rows.astype(jnp.float32) + step_offset[None, :])
    log_decay = -jnp.exp(decay_log)[None, :] * step_size
    feature_groups = group_spans(feature_conv, span_count, group_size)
    read_groups = group_spans(selector_conv[:, state_size:], span_count, group_size)
    write_groups = group_spans(selector_conv[:, :state_size], span_count, group_size)

    def run_terms(group_items):
        return jax.vmap(span_terms)(*group_items)

    pieces = (
        feature_groups,
        write_groups,
        read_groups,
        group_spans(step_size, span_count, group_size),
        group_spans(log_decay, span_count, group_size),
    )
    diagonal, cumulative, span_states, log_totals = lax.map(run_terms, pieces)
    span_states = ungroup(span_states, span_count)
    log_totals = ungroup(log_totals, span_count)
    entering, before, final_state, block_log = chain_states(span_states, log_totals)
    state_in = carry_fn(block_log, final_state)

    def one_span(diag_rows, cumul_rows, read_rows, state_local, log_before, feature_matrix_rows):
        length, head_count, head_width = diag_rows.shape
        entry_state = state_local + jnp.exp(log_before)[:, None, None] * state_in
        carried = jnp.einsum(
            "in,hnp->ihp",
            read_rows,
            entry_state.astype(jnp.bfloat16),
            preferred_element_type=jnp.float32,
        )
        head_view = feature_matrix_rows.reshape(length, head_count, head_width).astype(jnp.float32)
        summed = (
            diag_rows
            + jnp.exp(cumul_rows)[:, :, None] * carried
            + skip_scale[None, :, None] * head_view
        )
        return summed.reshape(length, head_count * head_width).astype(jnp.bfloat16)

    def run_output(group_items):
        return jax.vmap(one_span)(*group_items)

    regroup_entering = entering.reshape((span_count // group_size, group_size) + entering.shape[1:])
    regroup_before = before.reshape((span_count // group_size, group_size) + before.shape[1:])
    results = lax.map(
        run_output,
        (diagonal, cumulative, read_groups, regroup_entering, regroup_before, feature_groups),
    )
    return results.reshape(row_count, -1)


def token_conv(
    features, selector, feature_kernel, selector_kernel, feature_offset, selector_offset
):
    tail_count = feature_kernel.shape[0] - 1
    channels = features.shape[1]
    row_count = features.shape[0]
    last_rows = jnp.concatenate(
        [features[row_count - tail_count :], selector[row_count - tail_count :]], axis=1
    )
    tail_rows = passed_along(last_rows, ("seq", "head"), 1)
    feature_conv = causal_filter(tail_rows[:, :channels], features, feature_kernel, feature_offset)
    selector_conv = causal_filter(
        tail_rows[:, channels:], selector, selector_kernel, selector_offset
    )
    return (feature_conv, selector_conv)


def on_device(
    features,
    selector,
    step_input,
    feature_kernel,
    selector_kernel,
    feature_offset,
    selector_offset,
    decay_log,
    step_offset,
    skip_scale,
    norm_gain,
):
    head_count = decay_log.shape[0] // lax.axis_size("head")
    head_first = lax.axis_index("head") * head_count
    feature_send, selector_send = token_conv(
        features, selector, feature_kernel, selector_kernel, feature_offset, selector_offset
    )
    feature_slab, step_slab = (
        lax.all_to_all(feature_send, "head", split_axis=1, concat_axis=0, tiled=True),
        lax.all_to_all(step_input, "head", split_axis=1, concat_axis=0, tiled=True),
    )
    selector_slab = lax.all_gather(selector_send, "head", axis=0, tiled=True)
    feature_conv, selector_conv = (feature_slab, selector_slab)
    own_decay = lax.dynamic_slice_in_dim(decay_log, head_first, head_count, axis=0)
    own_step = lax.dynamic_slice_in_dim(step_offset, head_first, head_count, axis=0)
    own_skip = lax.dynamic_slice_in_dim(skip_scale, head_first, head_count, axis=0)

    def slab_prefix(block_log, final_state):
        prefix = entering_2(
            (block_log, final_state),
            "seq",
            join_states,
            (jnp.zeros_like(block_log), jnp.zeros_like(final_state)),
        )
        return prefix[1]

    mixed = selective_rows(
        feature_conv, selector_conv, step_slab, own_decay, own_step, own_skip, slab_prefix
    )
    blended_rows = lax.all_to_all(mixed, "head", split_axis=0, concat_axis=1, tiled=True)
    return normalize(blended_rows, norm_gain)


def solution(mesh):
    placed = (
        P(("seq", "head"), None),
        P(("seq", "head"), None),
        P(("seq", "head"), None),
        P(),
        P(),
        P(),
        P(),
        P(),
        P(),
        P(),
        P(),
    )
    return jax.shard_map(
        on_device, mesh=mesh, in_specs=placed, out_specs=P(("seq", "head"), None), check_vma=False
    )
```

profile of v0, /device:TPU:7, one launch (start us, length us, event | category | flops | bytes accessed | tf_op | source)
XLA Modules:
  0.0 1045.2 jit_solution(126070698641346954)
XLA Ops:
  20.9 16.6 %copy.85 = bf16[512,12288]{0,1:T(8,128)(2,1)} copy(bf16[512,12288]{1,0:T(8,128)(2,1)} %param.19) | data formatting | bytes 25165824 | tf_op args[0]
  39.8 17.2 %maximum_convert_fusion = f32[515,12288]{0,1:T(8,128)} fusion(bf16[512,12288]{0,1:T(8,128)(2,1)} %copy.85, bf16[3,12288]{0,1:T(8,128)(2,1)S(1)} %copy.84), kind=kLoop, calls=%fused_computation.78 | loop fusion | flops 25313280 | bytes 37969920 | tf_op jit(solution)/shard_map/convert_element_type | solution.py:38
  57.0 59.4 %multiply_convert_fusion.4 = bf16[512,12288]{0,1:T(8,128)(2,1)} fusion(f32[515,12288]{0,1:T(8,128)} %maximum_convert_fusion, f32[12288]{0:T(1024)S(1)} %bitcast.193, f32[12288]{0:T(1024)S(1)} %bitcast.194, f32[12288]{0:T(1024)S(1)} %bitcast.192, f32[12288]{0:T(1024)S(1)} %bitcast.191, f32[12288]{0:T(1024)S(1)} %copy-done.10), kind=kLoop, calls=%fused_computation.77 | loop fusion | flops 81788928 | bytes 113491968 | tf_op jit(solution)/shard_map/convert_element_type | solution.py:42
  124.9 238.1 %all-gather.5.cloned.1.call-done = bf16[4096,256]{1,0:T(8,128)(2,1)} async-done(((bf16[512,256]{1,0:T(8,128)(2,1)}), bf16[4096,256]{1,0:T(8,128)(2,1)}) %all-gather.5.cloned.1.call-update) | async-done | bytes 2097168 | tf_op jit(solution)/shard_map/all_gather | solution.py:193
  364.7 55.1 %all-to-all-done.1 = bf16[512,8,1536]{0,2,1:T(8,128)(2,1)} async-done(((bf16[512,8,1536]{0,2,1:T(8,128)(2,1)}), bf16[512,8,1536]{0,2,1:T(8,128)(2,1)}, u32[]{:S(2)}, u32[]{:S(2)}) %all-to-all-start.1) | async-done | bytes 12582944 | tf_op jit(solution)/shard_map/all_to_all | solution.py:190
  419.9 16.7 %copy.86 = bf16[8,512,1536]{2,1,0:T(8,128)(2,1)} copy(bf16[8,512,1536]{1,2,0:T(8,128)(2,1)} %bitcast.40) | data formatting | bytes 25165824 | tf_op jit(solution)/shard_map/all_to_all | solution.py:190
  436.5 15.7 %copy.89 = bf16[2,8,256,1536]{2,3,1,0:T(8,128)(2,1)} copy(bf16[2,8,256,1536]{3,2,1,0:T(8,128)(2,1)} %bitcast.181) | data formatting | bytes 25165824 | tf_op jit(solution)/shard_map/while | solution.py:119
  452.2 76.1 %while.51 = (s32[]{:T(128)}, f32[2,8,256,12,128]{2,4,3,1,0:T(8,128)}, f32[2,8,256,12]{2,1,3,0:T(8,128)}, f32[2,8,12,128,128]{4,3,2,1,0:T(8,128)}, f32[2,8,12]{2,...) while((s32[]{:T(128)}, ...), condition=%wide.region_3.4_spmd, body=%wide.region_0.3_spmd.sunk | while | flops 2597437696 | bytes 77813640 | solution.py:119
  462.4 9.7 bitcast_dynamic-update-slice_fusion.8
  500.4 9.7 bitcast_dynamic-update-slice_fusion.8
  528.3 36.3 %while.54 = (s32[]{:T(128)}, f32[12,128,128]{2,1,0:T(8,128)S(1)}, f32[16,12,128,128]{3,2,1,0:T(8,128)}, f32[16,12]{1,0:T(8,128)S(1)}, f32[16,12,128,128]{3,2,1,0:T(8,128)}, /*index=5*/s32[]{:T(128)}, s32[]{:T(128)}) while((s32[]{:T(128)}, f32[12,128,128]{2,1,0:T(8,128)S(1)}, f32[16,12,128,128]{3,2,1,0:T(8,128)}, ...), condition=%wide.region_5.6_spmd.clone, body=%wide.region_4.5_spmd.clone.sunk | while | flops 786435 | bytes 3932912 | solution.py:89
  573.5 10.8 %all-gather.7.cloned.1.call-done = bf16[48,128,128]{2,1,0:T(8,128)(2,1)} async-done(((bf16[12,128,128]{2,1,0:T(8,128)(2,1)}), bf16[48,128,128]{2,1,0:T(8,128)(2,1)}) %all-gather.7.cloned.1.call-update) | async-done | bytes 1572880 | tf_op jit(solution)/shard_map/all_gather | solution.py:19
  588.7 94.6 %while.53 = (s32[]{:T(128)}, bf16[2,8,256,1536]{3,2,1,0:T(8,128)(2,1)}, f32[2,8,256,12,128]{2,4,3,1,0:T(8,128)}, f32[2,8,256,12]{2,1,3,0:T(8,128)S(1)}, bf16[2,8...) while((s32[]{:T(128)}, ...), condition=%wide.region_11.12_spmd, body=%wide.region_10.11_spmd.sunk | while | flops 828899328 | bytes 142313392 | solution.py:147
  610.8 10.5 %fusion.86 = bf16[8,256,12,128]{1,3,2,0:T(8,128)(2,1)} fusion(bf16[8,256,12,128]{1,3,2,0:T(8,128)(2,1)S(1)} %bitcast.176, f32[8,256,12,128]{1,3,2,0:T(8,128)S(1)} %bitcast.173, f32[2,8,256,12,128]{2,4,3,1,0:T(8,128)} %get-tuple-element.654, s32[]{:T(128)} %get-tuple-element.641, f32[12]{0:T(128)S(1)} %get-tuple-element.660, f32[8,256,12]{1,2,0:T(8,128)S(1)} %fusion.85), kind=kLoop, calls=%fused_computation.43.clone.1 | loop fusion | flops 18874368 | bytes 37847092 | tf_op jit(solution)/shard_map/while/body/eval_jaxpr/vmap()/convert_element_type | solution.py:140
  621.3 8.8 copy.146
  636.0 6.9 constant_dynamic-slice_fusion.11
  658.1 10.5 %fusion.86 = bf16[8,256,12,128]{1,3,2,0:T(8,128)(2,1)} fusion(bf16[8,256,12,128]{1,3,2,0:T(8,128)(2,1)S(1)} %bitcast.176, f32[8,256,12,128]{1,3,2,0:T(8,128)S(1)} %bitcast.173, f32[2,8,256,12,128]{2,4,3,1,0:T(8,128)} %get-tuple-element.654, s32[]{:T(128)} %get-tuple-element.641, f32[12]{0:T(128)S(1)} %get-tuple-element.660, f32[8,256,12]{1,2,0:T(8,128)S(1)} %fusion.85), kind=kLoop, calls=%fused_computation.43.clone.1 | loop fusion | flops 18874368 | bytes 37847092 | tf_op jit(solution)/shard_map/while/body/eval_jaxpr/vmap()/convert_element_type | solution.py:140
  668.6 8.8 copy.146
  683.2 278.8 %all_to_all.42 = bf16[8,512,1536]{2,1,0:T(8,128)(2,1)S(1)} all-to-all(bf16[8,512,1536]{2,1,0:T(8,128)(2,1)} %bitcast.187), channel_id=1, replica_groups=mesh['seq'=4,'head'=8] {'head'}, dimensions={0} | all-to-all | bytes 25165824 | tf_op jit(solution)/shard_map/all_to_all | solution.py:211
  966.8 9.4 convert_bitcast_fusion
  976.2 24.7 %copy.97 = f32[512,8,1536]{0,2,1:T(8,128)} copy(f32[512,8,1536]{2,0,1:T(8,128)} %convert_bitcast_fusion) | data formatting | bytes 50331648 | tf_op jit(solution)/shard_map/convert_element_type | solution.py:46
  1000.9 7.1 fusion.40
  1008.1 13.7 %fusion.46 = bf16[512,12288]{0,1:T(8,128)(2,1)} fusion(f32[512,8,1536]{0,2,1:T(8,128)} %copy.97, f32[12288]{0:T(1024)S(1)} %copy-done.11, f32[512]{0:T(512)S(1)} %add_rsqrt_fusion), kind=kLoop, calls=%fused_computation.76 | loop fusion | flops 18874368 | bytes 37799936 | tf_op jit(solution)/shard_map/convert_element_type | solution.py:48
  1021.8 16.6 %copy.98 = bf16[512,12288]{1,0:T(8,128)(2,1)} copy(bf16[512,12288]{0,1:T(8,128)(2,1)} %fusion.46) | data formatting | bytes 25165824 | tf_op jit(solution)/shard_map/convert_element_type | solution.py:48
  (213 shorter events, 189.1 us)
Async XLA Ops:
  8.1 108.3 %all-to-all-start = ((bf16[512,8,12]{0,2,1:T(8,128)(2,1)}), bf16[512,8,12]{0,2,1:T(8,128)(2,1)S(1)}, u32[]{:S(2)}, u32[]{:S(2)}) async-start(bf16[512,8,12]{0,2,1:T(8,128)(2,1)} %all_to_all.32), calls=%async_computation | async-start | bytes 262144 | tf_op jit(solution)/shard_map/all_to_all | solution.py:191
  15.6 21.9 %collective-permute-start = (bf16[3,12544]{1,0:T(4,128)(2,1)S(1)}, bf16[3,12544]{1,0:T(4,128)(2,1)S(1)}, u32[]{:S(2)}, u32[]{:S(2)}) collective-permute-start(bf16[3,12544]{1,0:T(4,128)(2,1)S(1)} %pad_maximum_fusion), channel_id=1, source_target_pairs={{0,1},{1,2},{2,3},{3,4},{4,5},{5,6},{6,7},{7,8},{8,9},{9,10},{10,1... | collective-permute-start | bytes 225800 | tf_op jit(solution)/shard_map/ppermute | solution.py:13
  39.8 17.2 %copy-start.8 = (f32[1,12288]{1,0:T(1,128)S(1)}, f32[1,12288]{1,0:T(1,128)}, u32[]{:S(2)}) copy-start(f32[1,12288]{1,0:T(1,128)} %get-tuple-element.351) | copy-start | bytes 147460
  39.8 17.2 %copy-start.10 = (f32[12288]{0:T(1024)S(1)}, f32[12288]{0:T(1024)}, u32[]{:S(2)}) copy-start(f32[12288]{0:T(1024)} %param.24) | copy-start | bytes 147460
  116.4 5.8 copy-start.7
  116.5 5.8 copy-start.13
  116.5 7.2 copy-start.14
  116.5 7.3 copy-start.15
  116.5 303.4 %all-to-all-start.1 = ((bf16[512,8,1536]{0,2,1:T(8,128)(2,1)}), bf16[512,8,1536]{0,2,1:T(8,128)(2,1)}, u32[]{:S(2)}, u32[]{:S(2)}) async-start(bf16[512,8,1536]{0,2,1:T(8,128)(2,1)} %bitcast.180), calls=%async_computation.1 | async-start | bytes 25165824 | tf_op jit(solution)/shard_map/all_to_all | solution.py:190
  122.2 240.9 %all-gather.5.cloned.1.call-start = ((), (), s32[]{:S(2)}) async-start(), calls=%async_computation.3 | async-start | bytes 2359296 | tf_op jit(solution)/shard_map/all_gather | solution.py:193
  123.4 461.0 %all-gather.7.cloned.1.call-start = ((), (), s32[]{:S(2)}) async-start(), calls=%async_computation.4 | async-start | bytes 1966080 | tf_op jit(solution)/shard_map/all_gather | solution.py:19
  452.2 76.1 %copy-start.1 = (f32[12,128,128]{2,1,0:T(8,128)S(1)}, f32[12,128,128]{2,1,0:T(8,128)}, u32[]{:S(2)}) copy-start(f32[12,128,128]{2,1,0:T(8,128)} %custom-call) | copy-start | bytes 2359300
  528.3 37.2 %copy-start.16 = (f32[96]{0:T(128)S(1)}, f32[96]{0:T(128)}, u32[]{:S(2)}) copy-start(f32[96]{0:T(128)} %param.28) | copy-start | bytes 1156
  528.3 37.2 %copy-start.17 = (u32[32]{0:T(128)S(1)}, u32[32]{0:T(128)}, u32[]{:S(2)}) copy-start(u32[32]{0:T(128)} %constant.111) | copy-start | bytes 388
  528.3 60.4 %copy-start.6 = (f32[2,8,256,12]{2,1,3,0:T(8,128)S(1)}, f32[2,8,256,12]{2,1,3,0:T(8,128)}, u32[]{:S(2)}) copy-start(f32[2,8,256,12]{2,1,3,0:T(8,128)} %get-tuple-element.633) | copy-start | bytes 589828
  588.7 13.4 %copy-start.4 = (f32[12,128,128]{1,2,0:T(8,128)}, f32[12,128,128]{1,2,0:T(8,128)S(1)}, u32[]{:S(2)}) copy-start(f32[12,128,128]{1,2,0:T(8,128)S(1)} %get-tuple-element.659) | copy-start | bytes 2359300 | tf_op jit(solution)/shard_map/while
  588.7 17.0 %copy-start.2 = (bf16[2,8,256,128]{3,2,1,0:T(8,128)(2,1)}, bf16[2,8,256,128]{3,2,1,0:T(8,128)(2,1)S(1)}, u32[]{:S(2)}) copy-start(bf16[2,8,256,128]{3,2,1,0:T(8,128)(2,1)S(1)} %get-tuple-element.656) | copy-start | bytes 3145732 | tf_op jit(solution)/shard_map/while
  621.3 14.7 %copy-start.3 = (bf16[2,8,256,128]{3,2,1,0:T(8,128)(2,1)S(1)}, bf16[2,8,256,128]{3,2,1,0:T(8,128)(2,1)}, u32[]{:S(2)}) copy-start(bf16[2,8,256,128]{3,2,1,0:T(8,128)(2,1)} %copy-done.2) | copy-start | bytes 3145732 | tf_op jit(solution)/shard_map/while
  621.3 14.7 %copy-start.5 = (f32[12,128,128]{1,2,0:T(8,128)S(1)}, f32[12,128,128]{1,2,0:T(8,128)}, u32[]{:S(2)}) copy-start(f32[12,128,128]{1,2,0:T(8,128)} %copy-done.4) | copy-start | bytes 2359300 | tf_op jit(solution)/shard_map/while
  636.0 13.4 %copy-start.4 = (f32[12,128,128]{1,2,0:T(8,128)}, f32[12,128,128]{1,2,0:T(8,128)S(1)}, u32[]{:S(2)}) copy-start(f32[12,128,128]{1,2,0:T(8,128)S(1)} %get-tuple-element.659) | copy-start | bytes 2359300 | tf_op jit(solution)/shard_map/while
  636.0 17.0 %copy-start.2 = (bf16[2,8,256,128]{3,2,1,0:T(8,128)(2,1)}, bf16[2,8,256,128]{3,2,1,0:T(8,128)(2,1)S(1)}, u32[]{:S(2)}) copy-start(bf16[2,8,256,128]{3,2,1,0:T(8,128)(2,1)S(1)} %get-tuple-element.656) | copy-start | bytes 3145732 | tf_op jit(solution)/shard_map/while
  668.5 14.7 %copy-start.3 = (bf16[2,8,256,128]{3,2,1,0:T(8,128)(2,1)S(1)}, bf16[2,8,256,128]{3,2,1,0:T(8,128)(2,1)}, u32[]{:S(2)}) copy-start(bf16[2,8,256,128]{3,2,1,0:T(8,128)(2,1)} %copy-done.2) | copy-start | bytes 3145732 | tf_op jit(solution)/shard_map/while
  668.6 14.7 %copy-start.5 = (f32[12,128,128]{1,2,0:T(8,128)S(1)}, f32[12,128,128]{1,2,0:T(8,128)}, u32[]{:S(2)}) copy-start(f32[12,128,128]{1,2,0:T(8,128)} %copy-done.4) | copy-start | bytes 2359300 | tf_op jit(solution)/shard_map/while
  1000.9 7.1 copy-start.11
  (4 other events, 16.9 us)
Sparse Core Ops, SparseCore 0:
  125.1 237.8 all-gather.4
  565.5 18.8 all-gather.6
where the time goes:
time: 1050 us
  waiting for transfers between devices  304 us (29%)
  blocking collectives  285 us (27%)
  local copies, waits for them, and re-layouts  204 us (19%)
  other arithmetic  189 us (18%)
  matrix products  32.8 us (3%)
  starting transfers between devices  14.8 us (1%)
  between operations  14.4 us (1%)
    all_to_all x1, blocking collectives, on_device(): lax.all_to_all(mixed, 'head', split_axis=0, concat_axis=1, tiled=True)  279 us
    all_gather x1, waiting for transfers between devices, on_device(): selector_slab = lax.all_gather(selector_send, 'head', axis=0, tiled=True)  238 us
    convert_element_type x2, other arithmetic, causal_filter(): return jax.nn.silu(summed).astype(jnp.bfloat16)  60.5 us
    all_to_all x1, waiting for transfers between devices, on_device(): lax.all_to_all(feature_send, 'head', split_axis=1, concat_axis=0, tiled=T...  55.1 us
    dynamic_update_slice x4, local copies, waits for them, and re-layouts, selective_rows(): lax.map(run_output, (diagonal, cumulative, read_groups, regroup_entering,...  29.4 us
    dynamic_update_slice x8, local copies, waits for them, and re-layouts, selective_rows(): diagonal, cumulative, span_states, log_totals = lax.map(run_terms, pieces)  27 us
    dynamic_slice x4, local copies, waits for them, and re-layouts, selective_rows(): lax.map(run_output, (diagonal, cumulative, read_groups, regroup_entering,...  26.8 us
    convert_element_type x1, local copies, waits for them, and re-layouts, normalize(): widened = values.astype(jnp.float32)  24.7 us
  transfers between devices with their start and end apart: 5, of which 3 were waited for; matrix products, arithmetic and copies ran while one was open for 10% of the time, Pallas kernels for 0%

commit v1 on v0

--- a/solution.py
+++ b/solution.py
@@ -5,6 +5,28 @@
 from jax.sharding import PartitionSpec as P
 
 SPAN = 256
+
+
+def cut_along(value, dim, count):
+    before, after = (value.shape[:dim], value.shape[dim + 1 :])
+    return jnp.moveaxis(value.reshape(*before, count, -1, *after), dim, 0)
+
+
+def in_order(blocks, dim):
+    shape = list(blocks.shape[1:])
+    shape[dim] *= blocks.shape[0]
+    return jnp.moveaxis(blocks, 0, dim).reshape(shape)
+
+
+def swapped_with_each(array, axis, split_dim, concat_dim):
+    size, place = (lax.axis_size(axis), lax.axis_index(axis))
+    pieces = cut_along(array, split_dim, size)
+    outs = [pieces[place]]
+    for step in range(1, size):
+        sent = pieces[place ^ step]
+        outs.append(lax.ppermute(sent, axis, [(i, i ^ step) for i in range(size)]))
+    pieces = jnp.stack(outs)[place ^ jnp.arange(size)]
+    return in_order(pieces, concat_dim)
 
 
 def passed_along(shard, axis, by):
@@ -187,7 +209,7 @@
         features, selector, feature_kernel, selector_kernel, feature_offset, selector_offset
     )
     feature_slab, step_slab = (
-        lax.all_to_all(feature_send, "head", split_axis=1, concat_axis=0, tiled=True),
+        swapped_with_each(feature_send, "head", 1, 0),
         lax.all_to_all(step_input, "head", split_axis=1, concat_axis=0, tiled=True),
     )
     selector_slab = lax.all_gather(selector_send, "head", axis=0, tiled=True)

time: 1050 us -> 1060 us (level)
  waiting for transfers between devices: 304 us -> 267 us
  local copies, waits for them, and re-layouts: 204 us -> 238 us
  blocking collectives: 285 us -> 296 us
    all_gather x1, waiting for transfers between devices: 238 us -> 0.01 us  [on_device(): selector_slab = lax.all_gather(selector_send, 'head', axis=0, tiled=True)]
    ppermute x0 -> x7, waiting for transfers between devices: none -> 184 us  [swapped_with_each(): outs.append(lax.ppermute(sent, axis, [(i, i ^ step) for i in range(size)]))]
    all_gather x1, waiting for transfers between devices: 10.8 us -> 83.2 us  [entering_2(): lax.all_gather(a.astype(kind), axis)]
    all_to_all x1 -> x0, waiting for transfers between devices: 55.1 us -> none  [on_device(): lax.all_to_all(feature_send, 'head', split_axis=1, concat_axis=0, tiled=T...]
    another operation x9 -> x19, local copies, waits for them, and re-layouts: 0.27 us -> 22.4 us
    all_to_all x1 -> x0, local copies, waits for them, and re-layouts: 16.7 us -> none  [on_device(): lax.all_to_all(feature_send, 'head', split_axis=1, concat_axis=0, tiled=T...]
    unnamed x32 -> x39, local copies, waits for them, and re-layouts: 22.9 us -> 39 us
    gather x0 -> x1, local copies, waits for them, and re-layouts: none -> 11 us  [swapped_with_each(): pieces = jnp.stack(outs)[place ^ jnp.arange(size)]]
  transfers between devices with their start and end apart: 5 -> 11, of which waited for: 3 -> 5; matrix products, arithmetic and copies ran while one was open for 10% -> 16% of each run, Pallas kernels for 0% -> 0%
where the time goes in v1:
time: 1060 us
  blocking collectives  296 us (28%)
  waiting for transfers between devices  267 us (25%)
  local copies, waits for them, and re-layouts  238 us (22%)
  other arithmetic  191 us (18%)
  matrix products  32.6 us (3%)
  starting transfers between devices  18.9 us (2%)
  between operations  14.3 us (1%)
    all_to_all x1, blocking collectives, on_device(): lax.all_to_all(mixed, 'head', split_axis=0, concat_axis=1, tiled=True)  279 us
    ppermute x7, waiting for transfers between devices, swapped_with_each(): outs.append(lax.ppermute(sent, axis, [(i, i ^ step) for i in range(size)]))  184 us
    all_gather x1, waiting for transfers between devices, entering_2(): lax.all_gather(a.astype(kind), axis)  83.2 us
    convert_element_type x2, other arithmetic, causal_filter(): return jax.nn.silu(summed).astype(jnp.bfloat16)  61.7 us
    unnamed x39, local copies, waits for them, and re-layouts  39 us
    dynamic_update_slice x4, local copies, waits for them, and re-layouts, selective_rows(): lax.map(run_output, (diagonal, cumulative, read_groups, regroup_entering,...  29.5 us
    dynamic_update_slice x8, local copies, waits for them, and re-layouts, selective_rows(): diagonal, cumulative, span_states, log_totals = lax.map(run_terms, pieces)  27.2 us
    dynamic_slice x4, local copies, waits for them, and re-layouts, selective_rows(): lax.map(run_output, (diagonal, cumulative, read_groups, regroup_entering,...  26.9 us
  transfers between devices with their start and end apart: 11, of which 5 were waited for; matrix products, arithmetic and copies ran while one was open for 16% of the time, Pallas kernels for 0%

profile of v1, /device:TPU:7, one launch (start us, length us, event | category | flops | bytes accessed | tf_op | source)
XLA Modules:
  0.0 1058.3 jit_solution(2946174282600384753)
XLA Ops:
  17.8 16.7 %copy.92 = bf16[512,12288]{0,1:T(8,128)(2,1)} copy(bf16[512,12288]{1,0:T(8,128)(2,1)} %param.19) | data formatting | bytes 25165824 | tf_op args[0]
  38.9 17.2 %maximum_convert_fusion = f32[515,12288]{0,1:T(8,128)} fusion(bf16[512,12288]{0,1:T(8,128)(2,1)} %copy.92, bf16[3,12288]{0,1:T(8,128)(2,1)S(1)} %copy.91), kind=kLoop, calls=%fused_computation.79 | loop fusion | flops 25313280 | bytes 37969920 | tf_op jit(solution)/shard_map/convert_element_type | solution.py:60
  56.2 60.0 %multiply_convert_fusion.4 = bf16[512,12288]{0,1:T(8,128)(2,1)S(1)} fusion(f32[515,12288]{0,1:T(8,128)} %maximum_convert_fusion, f32[12288]{0:T(1024)S(1)} %bitcast.221, f32[12288]{0:T(1024)S(1)} %bitcast.222, f32[12288]{0:T(1024)S(1)} %bitcast.220, f32[12288]{0:T(1024)S(1)} %bitcast.219, f32[12288]{0:T(1024)S(1)} %copy-done.11), kind=kLoop, calls=%fused_computation.78 | loop fusion | flops 81788928 | bytes 113491968 | tf_op jit(solution)/shard_map/convert_element_type | solution.py:64
  161.9 67.3 %collective-permute-done.2 = bf16[512,1536]{1,0:T(8,128)(2,1)} collective-permute-done((bf16[512,1536]{1,0:T(8,128)(2,1)}, bf16[512,1536]{1,0:T(8,128)(2,1)}, u32[]{:S(2)}, u32[]{:S(2)}) %collective-permute-start.2) | collective-permute-done | bytes 1572896 | tf_op jit(solution)/shard_map/ppermute | solution.py:27
  234.7 30.0 %collective-permute-done.3 = bf16[512,1536]{1,0:T(8,128)(2,1)} collective-permute-done((bf16[512,1536]{1,0:T(8,128)(2,1)}, bf16[512,1536]{1,0:T(8,128)(2,1)}, u32[]{:S(2)}, u32[]{:S(2)}) %collective-permute-start.3) | collective-permute-done | bytes 1572896 | tf_op jit(solution)/shard_map/ppermute | solution.py:27
  270.1 77.6 %collective-permute-done.5 = bf16[512,1536]{1,0:T(8,128)(2,1)} collective-permute-done((bf16[512,1536]{1,0:T(8,128)(2,1)}, bf16[512,1536]{1,0:T(8,128)(2,1)}, u32[]{:S(2)}, u32[]{:S(2)}) %collective-permute-start.5) | collective-permute-done | bytes 1572896 | tf_op jit(solution)/shard_map/ppermute | solution.py:27
  353.0 11.0 %gather_fusion = bf16[8,512,1536]{2,1,0:T(8,128)(2,1)} fusion(bf16[8,512,1536]{2,1,0:T(8,128)(2,1)} %bitcast_dynamic-update-slice_fusion.4, s32[1024]{0:T(1024)S(1)} %pad_clamp_fusion), kind=kCustom, calls=%fused_computation | custom fusion | bytes 25165856 | tf_op jit(solution)/shard_map/gather | solution.py:28
  364.0 16.6 %copy.103 = bf16[2,8,256,1536]{2,3,1,0:T(8,128)(2,1)} copy(bf16[2,8,256,1536]{3,2,1,0:T(8,128)(2,1)} %bitcast.205) | data formatting | bytes 25165824 | tf_op jit(solution)/shard_map/while | solution.py:141
  382.4 76.0 %while.51 = (s32[]{:T(128)}, f32[2,8,256,12,128]{2,4,3,1,0:T(8,128)}, f32[2,8,256,12]{2,1,3,0:T(8,128)}, f32[2,8,12,128,128]{4,3,2,1,0:T(8,128)}, f32[2,8,12]{2,...) while((s32[]{:T(128)}, ...), condition=%wide.region_3.4_spmd, body=%wide.region_0.3_spmd.sunk | while | flops 2597437696 | bytes 77813640 | solution.py:141
  392.6 9.7 bitcast_dynamic-update-slice_fusion.16
  430.6 9.6 bitcast_dynamic-update-slice_fusion.16
  458.4 36.3 %while.54 = (s32[]{:T(128)}, f32[12,128,128]{2,1,0:T(8,128)S(1)}, f32[16,12,128,128]{3,2,1,0:T(8,128)}, f32[16,12]{1,0:T(8,128)S(1)}, f32[16,12,128,128]{3,2,1,0:T(8,128)}, /*index=5*/s32[]{:T(128)}, s32[]{:T(128)}) while((s32[]{:T(128)}, f32[12,128,128]{2,1,0:T(8,128)S(1)}, f32[16,12,128,128]{3,2,1,0:T(8,128)}, ...), condition=%wide.region_5.6_spmd.clone, body=%wide.region_4.5_spmd.clone.sunk | while | flops 786435 | bytes 3932912 | solution.py:111
  497.3 16.9 %all-reduce = bf16[48]{0:T(256)(128)(2,1)S(1)} all-reduce(bf16[48]{0:T(256)(128)(2,1)S(1)} %dynamic-update-slice), channel_id=2, replica_groups=mesh['seq'=4,'head'=8] {'seq'}, use_global_device_ids=true, to_apply=%add | all-reduce | flops 48 | bytes 192
  514.3 83.2 %all-gather.7.cloned.1.call-done = bf16[48,128,128]{2,1,0:T(8,128)(2,1)} async-done(((bf16[12,128,128]{2,1,0:T(8,128)(2,1)}), bf16[48,128,128]{2,1,0:T(8,128)(2,1)}) %all-gather.7.cloned.1.call-update) | async-done | bytes 1572880 | tf_op jit(solution)/shard_map/all_gather | solution.py:41
  601.8 94.6 %while.53 = (s32[]{:T(128)}, bf16[2,8,256,1536]{3,2,1,0:T(8,128)(2,1)}, f32[2,8,256,12,128]{2,4,3,1,0:T(8,128)}, f32[2,8,256,12]{2,1,3,0:T(8,128)S(1)}, bf16[2,8...) while((s32[]{:T(128)}, ...), condition=%wide.region_11.12_spmd, body=%wide.region_10.11_spmd.sunk | while | flops 828899328 | bytes 142313392 | solution.py:169
  623.9 10.4 fusion.87
  634.3 8.8 copy.160
  671.2 10.4 fusion.87
  681.6 8.8 copy.160
  696.4 278.8 %all_to_all.26 = bf16[8,512,1536]{2,1,0:T(8,128)(2,1)S(1)} all-to-all(bf16[8,512,1536]{2,1,0:T(8,128)(2,1)} %bitcast.211), channel_id=1, replica_groups=mesh['seq'=4,'head'=8] {'head'}, dimensions={0} | all-to-all | bytes 25165824 | tf_op jit(solution)/shard_map/all_to_all | solution.py:233
  979.9 9.4 convert_bitcast_fusion
  989.3 24.8 %copy.111 = f32[512,8,1536]{0,2,1:T(8,128)} copy(f32[512,8,1536]{2,0,1:T(8,128)} %convert_bitcast_fusion) | data formatting | bytes 50331648 | tf_op jit(solution)/shard_map/convert_element_type | solution.py:68
  1021.2 13.7 %fusion.46 = bf16[512,12288]{0,1:T(8,128)(2,1)} fusion(f32[512,8,1536]{0,2,1:T(8,128)} %copy.111, f32[12288]{0:T(1024)S(1)} %copy-done.12, f32[512]{0:T(512)S(1)} %add_rsqrt_fusion), kind=kLoop, calls=%fused_computation.77 | loop fusion | flops 18874368 | bytes 37799936 | tf_op jit(solution)/shard_map/convert_element_type | solution.py:70
  1034.9 16.6 %copy.112 = bf16[512,12288]{1,0:T(8,128)(2,1)} copy(bf16[512,12288]{0,1:T(8,128)(2,1)} %fusion.46) | data formatting | bytes 25165824 | tf_op jit(solution)/shard_map/convert_element_type | solution.py:70
  (244 shorter events, 249.5 us)
Async XLA Ops:
  8.3 28.4 %collective-permute-start = (bf16[3,12544]{1,0:T(4,128)(2,1)S(1)}, bf16[3,12544]{1,0:T(4,128)(2,1)S(1)}, u32[]{:S(2)}, u32[]{:S(2)}) collective-permute-start(bf16[3,12544]{1,0:T(4,128)(2,1)S(1)} %pad_maximum_fusion), channel_id=1, source_target_pairs={{0,1},{1,2},{2,3},{3,4},{4,5},{5,6},{6,7},{7,8},{8,9},{9,10},{10,1... | collective-permute-start | bytes 225800 | tf_op jit(solution)/shard_map/ppermute | solution.py:35
  13.0 133.0 %all-to-all-start = ((bf16[512,8,12]{0,2,1:T(8,128)(2,1)}), bf16[512,8,12]{0,2,1:T(8,128)(2,1)S(1)}, u32[]{:S(2)}, u32[]{:S(2)}) async-start(bf16[512,8,12]{0,2,1:T(8,128)(2,1)} %all_to_all.20), calls=%async_computation | async-start | bytes 262144 | tf_op jit(solution)/shard_map/all_to_all | solution.py:213
  17.8 362.9 %all-gather.5.cloned.1.call-start = ((), (), s32[]{:S(2)}) async-start(), calls=%async_computation.2 | async-start | bytes 2359296 | tf_op jit(solution)/shard_map/all_gather | solution.py:215
  17.8 16.8 %copy-start.9 = (f32[4,12288]{1,0:T(4,128)S(1)}, f32[4,12288]{1,0:T(4,128)}, u32[]{:S(2)}) copy-start(f32[4,12288]{1,0:T(4,128)} %param.22) | copy-start | bytes 589828
  17.8 17.5 %copy-start.14 = (f32[96]{0:T(128)S(1)}, f32[96]{0:T(128)}, u32[]{:S(2)}) copy-start(f32[96]{0:T(128)} %param.27) | copy-start | bytes 1156
  17.8 18.2 %copy-start.15 = (f32[96]{0:T(128)S(1)}, f32[96]{0:T(128)}, u32[]{:S(2)}) copy-start(f32[96]{0:T(128)} %param.26) | copy-start | bytes 1156
  38.9 17.3 %copy-start.8 = (f32[1,12288]{1,0:T(1,128)S(1)}, f32[1,12288]{1,0:T(1,128)}, u32[]{:S(2)}) copy-start(f32[1,12288]{1,0:T(1,128)} %get-tuple-element.359) | copy-start | bytes 147460
  38.9 17.3 %copy-start.11 = (f32[12288]{0:T(1024)S(1)}, f32[12288]{0:T(1024)}, u32[]{:S(2)}) copy-start(f32[12288]{0:T(1024)} %param.24) | copy-start | bytes 147460
  121.5 34.8 %collective-permute-start.1 = (bf16[512,1536]{1,0:T(8,128)(2,1)}, bf16[512,1536]{1,0:T(8,128)(2,1)}, u32[]{:S(2)}, u32[]{:S(2)}) collective-permute-start(bf16[512,1536]{1,0:T(8,128)(2,1)} %bitcast.215), channel_id=1, source_target_pairs={{0,1},{1,0},{2,3},{3,2},{4,5},{5,4},{6,7},{7,6},{8,9},{9,8},{10,11... | collective-permute-start | bytes 4718600 | tf_op jit(solution)/shard_map/ppermute | solution.py:27
  122.3 21.6 %copy-start.7 = (bf16[512,256]{1,0:T(8,128)(2,1)S(1)}, bf16[512,256]{1,0:T(8,128)(2,1)}, u32[]{:S(2)}) copy-start(bf16[512,256]{1,0:T(8,128)(2,1)} %param.20) | copy-start | bytes 786436
  122.3 21.6 %slice-start = ((bf16[3,12544]{1,0:T(4,128)(2,1)}), bf16[3,256]{1,0:T(4,128)(2,1)S(1)}, s32[]{:S(2)}) async-start(bf16[3,12544]{1,0:T(4,128)(2,1)} %copy-done.10), calls=%async_computation.4 | async-start | bytes 4096 | tf_op jit(solution)/shard_map/slice | solution.py:188
  126.7 102.5 %collective-permute-start.2 = (bf16[512,1536]{1,0:T(8,128)(2,1)}, bf16[512,1536]{1,0:T(8,128)(2,1)}, u32[]{:S(2)}, u32[]{:S(2)}) collective-permute-start(bf16[512,1536]{1,0:T(8,128)(2,1)} %bitcast.216), channel_id=1, source_target_pairs={{0,2},{1,3},{2,0},{3,1},{4,6},{5,7},{6,4},{7,5},{8,10},{9,11},{10,... | collective-permute-start | bytes 4718600 | tf_op jit(solution)/shard_map/ppermute | solution.py:27
  132.0 132.8 %collective-permute-start.3 = (bf16[512,1536]{1,0:T(8,128)(2,1)}, bf16[512,1536]{1,0:T(8,128)(2,1)}, u32[]{:S(2)}, u32[]{:S(2)}) collective-permute-start(bf16[512,1536]{1,0:T(8,128)(2,1)} %bitcast.45), channel_id=1, source_target_pairs={{0,3},{1,2},{2,1},{3,0},{4,7},{5,6},{6,5},{7,4},{8,11},{9,10},{10,... | collective-permute-start | bytes 4718600 | tf_op jit(solution)/shard_map/ppermute | solution.py:27
  135.7 131.7 %collective-permute-start.4 = (bf16[512,1536]{1,0:T(8,128)(2,1)}, bf16[512,1536]{1,0:T(8,128)(2,1)}, u32[]{:S(2)}, u32[]{:S(2)}) collective-permute-start(bf16[512,1536]{1,0:T(8,128)(2,1)} %bitcast.47), channel_id=1, source_target_pairs={{0,4},{1,5},{2,6},{3,7},{4,0},{5,1},{6,2},{7,3},{8,12},{9,13},{10,... | collective-permute-start | bytes 4718600 | tf_op jit(solution)/shard_map/ppermute | solution.py:27
  140.4 207.3 %collective-permute-start.5 = (bf16[512,1536]{1,0:T(8,128)(2,1)}, bf16[512,1536]{1,0:T(8,128)(2,1)}, u32[]{:S(2)}, u32[]{:S(2)}) collective-permute-start(bf16[512,1536]{1,0:T(8,128)(2,1)} %bitcast.49), channel_id=1, source_target_pairs={{0,5},{1,4},{2,7},{3,6},{4,1},{5,0},{6,3},{7,2},{8,13},{9,12},{10,... | collective-permute-start | bytes 4718600 | tf_op jit(solution)/shard_map/ppermute | solution.py:27
  145.7 451.7 %all-gather.7.cloned.1.call-start = ((), (), s32[]{:S(2)}) async-start(), calls=%async_computation.3 | async-start | bytes 1966080 | tf_op jit(solution)/shard_map/all_gather | solution.py:41
  156.3 194.2 %collective-permute-start.6 = (bf16[512,1536]{1,0:T(8,128)(2,1)}, bf16[512,1536]{1,0:T(8,128)(2,1)S(1)}, u32[]{:S(2)}, u32[]{:S(2)}) collective-permute-start(bf16[512,1536]{1,0:T(8,128)(2,1)} %bitcast.214), channel_id=1, source_target_pairs={{0,6},{1,7},{2,4},{3,5},{4,2},{5,3},{6,0},{7,1},{8,14},{9,15},{10,... | collective-permute-start | bytes 4718600 | tf_op jit(solution)/shard_map/ppermute | solution.py:27
  229.2 122.5 %collective-permute-start.7 = (bf16[512,1536]{1,0:T(8,128)(2,1)S(1)}, bf16[512,1536]{1,0:T(8,128)(2,1)S(1)}, u32[]{:S(2)}, u32[]{:S(2)}) collective-permute-start(bf16[512,1536]{1,0:T(8,128)(2,1)S(1)} %bitcast.213), channel_id=1, source_target_pairs={{0,7},{1,6},{2,5},{3,4},{4,3},{5,2},{6,1},{7,0},{8,15},{9,14},{10,... | collective-permute-start | bytes 4718600 | tf_op jit(solution)/shard_map/ppermute | solution.py:27
  382.4 76.0 %copy-start.1 = (f32[12,128,128]{2,1,0:T(8,128)S(1)}, f32[12,128,128]{2,1,0:T(8,128)}, u32[]{:S(2)}) copy-start(f32[12,128,128]{2,1,0:T(8,128)} %custom-call) | copy-start | bytes 2359300
  458.4 37.2 %copy-start.16 = (f32[96]{0:T(128)S(1)}, f32[96]{0:T(128)}, u32[]{:S(2)}) copy-start(f32[96]{0:T(128)} %param.28) | copy-start | bytes 1156
  458.4 37.3 %copy-start.17 = (u32[32]{0:T(128)S(1)}, u32[32]{0:T(128)}, u32[]{:S(2)}) copy-start(u32[32]{0:T(128)} %constant.129) | copy-start | bytes 388
  458.4 143.3 %copy-start.6 = (f32[2,8,256,12]{2,1,3,0:T(8,128)S(1)}, f32[2,8,256,12]{2,1,3,0:T(8,128)}, u32[]{:S(2)}) copy-start(f32[2,8,256,12]{2,1,3,0:T(8,128)} %get-tuple-element.641) | copy-start | bytes 589828
  601.8 17.0 %copy-start.2 = (bf16[2,8,256,128]{3,2,1,0:T(8,128)(2,1)}, bf16[2,8,256,128]{3,2,1,0:T(8,128)(2,1)S(1)}, u32[]{:S(2)}) copy-start(bf16[2,8,256,128]{3,2,1,0:T(8,128)(2,1)S(1)} %get-tuple-element.664) | copy-start | bytes 3145732 | tf_op jit(solution)/shard_map/while
  649.1 17.0 %copy-start.2 = (bf16[2,8,256,128]{3,2,1,0:T(8,128)(2,1)}, bf16[2,8,256,128]{3,2,1,0:T(8,128)(2,1)S(1)}, u32[]{:S(2)}) copy-start(bf16[2,8,256,128]{3,2,1,0:T(8,128)(2,1)S(1)} %get-tuple-element.664) | copy-start | bytes 3145732 | tf_op jit(solution)/shard_map/while
  (10 other events, 104.0 us)
Sparse Core Ops, SparseCore 0:
  145.8 229.9 all-gather.4
  495.7 101.6 all-gather.6
